TPU v7x, 256 devices: a whole 4x4x8 slice. The times are simulated.
256 devices in a mesh: row: 8 (over z), col: 8 (over x, core), sub: 4 (over y).
Axes of the slice: x: 4, y: 4, z: 8, core: 2. Of those that a mesh axis runs over, the one named last changes fastest.
Arguments:
- front_entries: float32 [8192, 8192], P('row', ('col', 'sub')), may hold values from -1 to 4, as said below
- child_blocks: float32 [4, 2048, 2048], P('sub', 'row', 'col'), may hold values from -1 to 2, as said below
- child_map: int32 [4, 16], P('sub'), may hold values from 0 to 63, as said below
Outputs:
- factored: float32 [8192, 8192], P('row', ('col', 'sub'))
Inputs may be any that keep to these rules, and one draw needn't show every extreme that they name: Each row of child_map lists 16 different parent blocks in increasing order and ends with block 63. In natural order front_entries is a symmetric matrix, and the assembled front is positive definite. `child_blocks`: in natural order each child's contribution block is a symmetric matrix.
All inputs are finite; a program needn't handle non-finite values.
Results may differ from a plain program's by a relative error of at most 0.00005.
Values sent between devices are 32-bit elements; how exact they have to be, the bound alone decides.
A program may use at most 128 MiB of HBM per device.

v0:
```python
import jax
import jax.numpy as jnp
from jax import lax
from jax.sharding import PartitionSpec as P

BLK = 128
NPIV = 6
highest = lax.Precision.HIGHEST


def broadcast(value, axis, source):
    kept = jnp.where(lax.axis_index(axis) == source, value, 0).astype(value.dtype)
    return lax.psum(kept, axis)


def lookup(index_table, wanted):
    positions = jnp.arange(index_table.shape[0], dtype=jnp.int32)
    return jnp.sum(jnp.where(wanted[..., None] == positions, index_table, 0), axis=-1)


def body(front_entries, child_blocks, child_map):
    row_count = lax.axis_size("row")
    col_count = lax.axis_size("col")
    sub_count = lax.axis_size("sub")
    row_index = lax.axis_index("row")
    col_index = lax.axis_index("col")
    sub_index = lax.axis_index("sub")
    child_tile = child_blocks[0]
    mapping = child_map[0]
    local_rows = front_entries.shape[0]
    row_blocks = local_rows // BLK
    slot_count = front_entries.shape[1] // BLK
    col_blocks = slot_count * sub_count
    child_rows = child_tile.shape[0] // BLK
    child_cols = child_tile.shape[1] // BLK
    zero_carry = jnp.zeros((row_blocks, BLK, col_blocks, BLK), jnp.float32)
    incoming = lax.all_gather(child_tile[None], ("row", "col"), axis=0, tiled=True)
    piece_count = incoming.shape[0]
    source = jnp.arange(piece_count, dtype=jnp.int32)
    source_row = source // col_count
    source_col = source % col_count
    row_parent = lookup(
        mapping, jnp.arange(child_rows, dtype=jnp.int32)[None, :] * row_count + source_row[:, None]
    )
    col_parent = lookup(
        mapping, jnp.arange(child_cols, dtype=jnp.int32)[None, :] * col_count + source_col[:, None]
    )
    row_target = jnp.where(row_parent % row_count == row_index, row_parent // row_count, row_blocks)
    col_target = jnp.where(col_parent % col_count == col_index, col_parent // col_count, col_blocks)
    tile_stack = incoming.reshape(piece_count, child_rows, BLK, child_cols, BLK).transpose(
        0, 1, 3, 2, 4
    )
    spread_sum = zero_carry.at[row_target[:, :, None], :, col_target[:, None, :], :].add(
        tile_stack, mode="drop"
    )
    spread_sum = spread_sum.reshape(local_rows, col_blocks * BLK)
    summed = lax.psum_scatter(spread_sum, "sub", scatter_dimension=1, tiled=True)
    matrix = front_entries + summed
    row_global = jnp.repeat(jnp.arange(row_blocks, dtype=jnp.int32) * row_count + row_index, BLK)
    col_global = jnp.repeat(
        (sub_index * slot_count + jnp.arange(slot_count, dtype=jnp.int32)) * col_count + col_index,
        BLK,
    )
    for pivot_step in range(NPIV):
        sources_col_slot = pivot_step // col_count % slot_count
        sources_pivot_block = pivot_step // row_count
        col_source = matrix[:, sources_col_slot * BLK : (sources_col_slot + 1) * BLK]
        row_source = matrix[sources_pivot_block * BLK : (sources_pivot_block + 1) * BLK, :]
        root_group = pivot_step % col_count * sub_count + pivot_step // col_count // slot_count
        share_col_panel = broadcast(col_source, ("col", "sub"), root_group)
        pivot_block = pivot_step // row_count
        share_diagonal = share_col_panel[pivot_block * BLK : (pivot_block + 1) * BLK, :]
        share_pivot_row_panel, share_diagonal = (
            broadcast(row_source, "row", pivot_step % row_count),
            broadcast(share_diagonal, "row", pivot_step % row_count),
        )
        pivot_factor = jnp.linalg.cholesky(share_diagonal)
        lower_rows = jax.scipy.linalg.solve_triangular(
            pivot_factor, share_col_panel.T, lower=True
        ).T
        upper_rows = jax.scipy.linalg.solve_triangular(
            pivot_factor, share_pivot_row_panel, lower=True
        )
        left_factor = jnp.where(row_global[:, None] > pivot_step, lower_rows, 0.0)
        right_factor = jnp.where(col_global[None, :] > pivot_step, upper_rows, 0.0)
        factor_column = jnp.where(row_global[:, None] >= pivot_step, lower_rows, 0.0)
        left_factor, right_factor, column = (left_factor, right_factor, factor_column)
        matrix = matrix - jnp.dot(left_factor, right_factor, precision=highest)
        col_slot = pivot_step // col_count % slot_count
        is_owner = (col_index == pivot_step % col_count) & (
            sub_index == pivot_step // col_count // slot_count
        )
        existing = matrix[:, col_slot * BLK : (col_slot + 1) * BLK]
        matrix = matrix.at[:, col_slot * BLK : (col_slot + 1) * BLK].set(
            jnp.where(is_owner, column, existing)
        )
    upper_right = (row_global[:, None] < NPIV) & (col_global[None, :] >= NPIV)
    return jnp.where(upper_right, 0.0, matrix)


def solution(mesh):
    placed = (P("row", ("col", "sub")), P("sub", "row", "col"), P("sub", None))
    return jax.shard_map(
        body, mesh=mesh, in_specs=placed, out_specs=P("row", ("col", "sub")), check_vma=False
    )
```

profile of v0, /device:TPU:2, one launch (start us, length us, event | category | flops | bytes accessed | tf_op | source)
XLA Modules:
  0.0 1576.2 jit_solution(9138514772814132844)
XLA Ops:
  9.0 102.0 %all-gather.2.cloned.1.call-done = f32[64,256,256]{2,1,0:T(8,128)} async-done(((f32[1,256,256]{2,1,0:T(8,128)}), f32[64,256,256]{2,1,0:T(8,128)}) %all-gather.2.cloned.1.call-update) | async-done | bytes 16777232 | tf_op jit(solution)/shard_map/all_gather | solution.py:37
  111.0 20.8 %reshape.466 = f32[64,2,128,2,128]{4,3,2,1,0:T(2,128)} reshape(f32[64,256,256]{2,1,0:T(8,128)} %all-gather.2.cloned.1.call-done) | data formatting | bytes 33554432 | tf_op jit(solution)/shard_map/reshape | solution.py:50
  131.8 12.6 copy.62
  144.5 2.4 broadcast_in_dim.231
  146.9 49.3 %scatter_fusion = f32[8,128,8,128]{3,1,2,0:T(8,128)} fusion(f32[8,128,8,128]{3,1,2,0:T(8,128)} %broadcast_in_dim.231, s32[256]{0:T(256)S(1)} %reshape.468, f32[256,128,128]{2,1,0:T(8,128)} %bitcast.192), kind=kCustom, calls=%fused_computation | custom fusion | flops 4194304 | bytes 50333696 | tf_op jit(solution)/shard_map/scatter-add | solution.py:53
  196.2 5.5 copy.63
  201.7 5.2 copy.98
  208.1 48.3 %reduce-scatter.2.cloned.1.call-done = f32[1024,256]{0,1:T(8,128)} async-done(((f32[1024,1024]{0,1:T(8,128)}), f32[1024,256]{0,1:T(8,128)}) %reduce-scatter.2.cloned.1.call-update) | async-done | bytes 1048592 | tf_op jit(solution)/shard_map/reduce_scatter | solution.py:57
  260.1 113.2 %all-reduce.19.cloned.1.call-done = f32[1024,128]{0,1:T(8,128)} async-done(((f32[1024,128]{0,1:T(8,128)}), f32[1024,128]{0,1:T(8,128)}) %all-reduce.19.cloned.1.call-update) | async-done | bytes 524304 | tf_op jit(solution)/shard_map/psum | solution.py:13
  375.1 73.6 %all-reduce.41.cloned.1.call-done = (f32[128,256]{0,1:T(8,128)}, f32[128,128]{0,1:T(8,128)}) async-done(((f32[128,256]{0,1:T(8,128)}, f32[128,128]{0,1:T(8,128)}), (f32[128,256]{0,1:T(8,128)}, f32[128,128]{0,1:T(8,128)})) %all-reduce.41.cloned.1.call-update) | async-done | bytes 196624 | tf_op jit(solution)/shard_map/psum | solution.py:13
  450.4 11.7 cholesky.104
  463.5 9.8 custom-call.20
  479.6 111.7 %all-reduce.21.cloned.1.call-done = f32[1024,128]{0,1:T(8,128)} async-done(((f32[1024,128]{0,1:T(8,128)}), f32[1024,128]{0,1:T(8,128)}) %all-reduce.21.cloned.1.call-update) | async-done | bytes 524304 | tf_op jit(solution)/shard_map/psum | solution.py:13
  593.1 73.5 %all-reduce.39.cloned.1.call-done = (f32[128,256]{0,1:T(8,128)}, f32[128,128]{0,1:T(8,128)}) async-done(((f32[128,256]{0,1:T(8,128)}, f32[128,128]{0,1:T(8,128)}), (f32[128,256]{0,1:T(8,128)}, f32[128,128]{0,1:T(8,128)})) %all-reduce.39.cloned.1.call-update) | async-done | bytes 196624 | tf_op jit(solution)/shard_map/psum | solution.py:13
  668.4 11.7 cholesky.115
  681.5 9.8 custom-call.22
  697.5 111.7 %all-reduce.23.cloned.1.call-done = f32[1024,128]{0,1:T(8,128)} async-done(((f32[1024,128]{0,1:T(8,128)}), f32[1024,128]{0,1:T(8,128)}) %all-reduce.23.cloned.1.call-update) | async-done | bytes 524304 | tf_op jit(solution)/shard_map/psum | solution.py:13
  811.1 73.6 %all-reduce.37.cloned.1.call-done = (f32[128,256]{0,1:T(8,128)}, f32[128,128]{0,1:T(8,128)}) async-done(((f32[128,256]{0,1:T(8,128)}, f32[128,128]{0,1:T(8,128)}), (f32[128,256]{0,1:T(8,128)}, f32[128,128]{0,1:T(8,128)})) %all-reduce.37.cloned.1.call-update) | async-done | bytes 196624 | tf_op jit(solution)/shard_map/psum | solution.py:13
  886.5 11.7 cholesky.126
  899.6 9.8 custom-call.24
  915.7 111.7 %all-reduce.25.cloned.1.call-done = f32[1024,128]{0,1:T(8,128)} async-done(((f32[1024,128]{0,1:T(8,128)}), f32[1024,128]{0,1:T(8,128)}) %all-reduce.25.cloned.1.call-update) | async-done | bytes 524304 | tf_op jit(solution)/shard_map/psum | solution.py:13
  1029.4 73.3 %all-reduce.35.cloned.1.call-done = (f32[128,256]{0,1:T(8,128)}, f32[128,128]{0,1:T(8,128)}) async-done(((f32[128,256]{0,1:T(8,128)}, f32[128,128]{0,1:T(8,128)}), (f32[128,256]{0,1:T(8,128)}, f32[128,128]{0,1:T(8,128)})) %all-reduce.35.cloned.1.call-update) | async-done | bytes 196624 | tf_op jit(solution)/shard_map/psum | solution.py:13
  1104.5 11.7 cholesky.137
  1117.6 9.8 custom-call.26
  1133.7 111.7 %all-reduce.27.cloned.1.call-done = f32[1024,128]{0,1:T(8,128)} async-done(((f32[1024,128]{0,1:T(8,128)}), f32[1024,128]{0,1:T(8,128)}) %all-reduce.27.cloned.1.call-update) | async-done | bytes 524304 | tf_op jit(solution)/shard_map/psum | solution.py:13
  1247.1 73.6 %all-reduce.33.cloned.1.call-done = (f32[128,256]{0,1:T(8,128)}, f32[128,128]{0,1:T(8,128)}) async-done(((f32[128,256]{0,1:T(8,128)}, f32[128,128]{0,1:T(8,128)}), (f32[128,256]{0,1:T(8,128)}, f32[128,128]{0,1:T(8,128)})) %all-reduce.33.cloned.1.call-update) | async-done | bytes 196624 | tf_op jit(solution)/shard_map/psum | solution.py:13
  1322.5 11.7 cholesky.148
  1335.5 9.8 custom-call.28
  1351.8 111.5 %all-reduce.29.cloned.1.call-done = f32[1024,128]{0,1:T(8,128)} async-done(((f32[1024,128]{0,1:T(8,128)}), f32[1024,128]{0,1:T(8,128)}) %all-reduce.29.cloned.1.call-update) | async-done | bytes 524304 | tf_op jit(solution)/shard_map/psum | solution.py:13
  1464.9 73.8 %all-reduce.31.cloned.1.call-done = (f32[128,256]{0,1:T(8,128)}, f32[128,128]{0,1:T(8,128)}) async-done(((f32[128,256]{0,1:T(8,128)}, f32[128,128]{0,1:T(8,128)}), (f32[128,256]{0,1:T(8,128)}, f32[128,128]{0,1:T(8,128)})) %all-reduce.31.cloned.1.call-update) | async-done | bytes 196624 | tf_op jit(solution)/shard_map/psum | solution.py:13
  1540.5 11.7 cholesky.159
  1553.6 9.8 custom-call.30
  (149 shorter events, 74.2 us)
Async XLA Ops:
  6.5 104.5 %all-gather.2.cloned.1.call-start = ((), (), s32[]{:S(2)}) async-start(), calls=%async_computation.1 | async-start | bytes 17039360 | tf_op jit(solution)/shard_map/all_gather | solution.py:37
  7.3 249.2 %reduce-scatter.2.cloned.1.call-start = ((), (), s32[]{:S(2)}) async-start(), calls=%async_computation.2 | async-start | bytes 5242880 | tf_op jit(solution)/shard_map/reduce_scatter | solution.py:57
  196.2 10.7 copy-start
  206.9 166.4 %all-reduce.19.cloned.1.call-start = ((), (), s32[]{:S(2)}) async-start(), calls=%async_computation.3 | async-start | bytes 1048576 | tf_op jit(solution)/shard_map/psum | solution.py:13
  258.7 190.0 %all-reduce.41.cloned.1.call-start = ((), (), s32[]{:S(2)}) async-start(), calls=%async_computation.14 | async-start | bytes 393216 | tf_op jit(solution)/shard_map/psum | solution.py:13
  374.8 216.5 %all-reduce.21.cloned.1.call-start = ((), (), s32[]{:S(2)}) async-start(), calls=%async_computation.4 | async-start | bytes 1048576 | tf_op jit(solution)/shard_map/psum | solution.py:13
  478.8 187.8 %all-reduce.39.cloned.1.call-start = ((), (), s32[]{:S(2)}) async-start(), calls=%async_computation.13 | async-start | bytes 393216 | tf_op jit(solution)/shard_map/psum | solution.py:13
  592.7 216.5 %all-reduce.23.cloned.1.call-start = ((), (), s32[]{:S(2)}) async-start(), calls=%async_computation.5 | async-start | bytes 1048576 | tf_op jit(solution)/shard_map/psum | solution.py:13
  696.8 188.0 %all-reduce.37.cloned.1.call-start = ((), (), s32[]{:S(2)}) async-start(), calls=%async_computation.12 | async-start | bytes 393216 | tf_op jit(solution)/shard_map/psum | solution.py:13
  810.7 216.6 %all-reduce.25.cloned.1.call-start = ((), (), s32[]{:S(2)}) async-start(), calls=%async_computation.6 | async-start | bytes 1048576 | tf_op jit(solution)/shard_map/psum | solution.py:13
  914.9 187.8 %all-reduce.35.cloned.1.call-start = ((), (), s32[]{:S(2)}) async-start(), calls=%async_computation.11 | async-start | bytes 393216 | tf_op jit(solution)/shard_map/psum | solution.py:13
  1028.8 216.5 %all-reduce.27.cloned.1.call-start = ((), (), s32[]{:S(2)}) async-start(), calls=%async_computation.7 | async-start | bytes 1048576 | tf_op jit(solution)/shard_map/psum | solution.py:13
  1132.9 187.8 %all-reduce.33.cloned.1.call-start = ((), (), s32[]{:S(2)}) async-start(), calls=%async_computation.10 | async-start | bytes 393216 | tf_op jit(solution)/shard_map/psum | solution.py:13
  1246.8 216.5 %all-reduce.29.cloned.1.call-start = ((), (), s32[]{:S(2)}) async-start(), calls=%async_computation.8 | async-start | bytes 1048576 | tf_op jit(solution)/shard_map/psum | solution.py:13
  1350.8 187.9 %all-reduce.31.cloned.1.call-start = ((), (), s32[]{:S(2)}) async-start(), calls=%async_computation.9 | async-start | bytes 393216 | tf_op jit(solution)/shard_map/psum | solution.py:13
Sparse Core Ops, SparseCore 0:
  10.1 100.8 all-gather.1
  207.0 49.4 reduce-scatter.1
  259.6 113.5 all-reduce.18
  375.5 73.0 all-reduce.40
  478.9 112.2 all-reduce.20
  593.5 73.0 all-reduce.38
  696.9 112.2 all-reduce.22
  811.6 73.0 all-reduce.36
  915.0 112.2 all-reduce.24
  1029.6 73.0 all-reduce.34
  1133.0 112.2 all-reduce.26
  1247.5 73.0 all-reduce.32
  1351.0 112.3 all-reduce.28
  1465.6 73.0 all-reduce.30
where the time goes:
time: 1580 us
  waiting for transfers between devices  1260 us (80%)
  other arithmetic  217 us (14%)
  local copies, waits for them, and re-layouts  55.7 us (4%)
  matrix products  23.1 us (1%)
    psum x12, waiting for transfers between devices, broadcast(): return lax.psum(kept, axis)  1110 us
    all_gather x1, waiting for transfers between devices, body(): lax.all_gather(child_tile[None], ('row', 'col'), axis=0, tiled=True)  102 us
    another operation x18, other arithmetic, body(): pivot_factor = jnp.linalg.cholesky(share_diagonal)  74.3 us
    another operation x12, other arithmetic, body(): jax.scipy.linalg.solve_triangular(pivot_factor, share_col_panel.T, lower=...  62.8 us
    scatter-add x1, other arithmetic, body(): zero_carry.at[row_target[:, :, None], :, col_target[:, None, :], :]  49.3 us
    reduce_scatter x1, waiting for transfers between devices, body(): lax.psum_scatter(spread_sum, 'sub', scatter_dimension=1, tiled=True)  48.3 us
  transfers between devices with their start and end apart: 14, of which 14 were waited for; matrix products, arithmetic and copies ran while one was open for 1% of the time, Pallas kernels for 0%

commit v1 on v0

--- a/solution.py
+++ b/solution.py
@@ -34,7 +34,12 @@
     child_rows = child_tile.shape[0] // BLK
     child_cols = child_tile.shape[1] // BLK
     zero_carry = jnp.zeros((row_blocks, BLK, col_blocks, BLK), jnp.float32)
-    incoming = lax.all_gather(child_tile[None], ("row", "col"), axis=0, tiled=True)
+    incoming = jnp.concatenate(
+        lax.all_to_all(
+            jnp.stack([child_tile[None]] * lax.axis_size(("row", "col"))), ("row", "col"), 0, 0
+        ),
+        axis=0,
+    )
     piece_count = incoming.shape[0]
     source = jnp.arange(piece_count, dtype=jnp.int32)
     source_row = source // col_count

time: 1580 us -> 1870 us (1.18)
  waiting for transfers between devices: 1260 us -> 1530 us
    all_to_all x0 -> x1, waiting for transfers between devices: none -> 368 us  [body(): lax.all_to_all(jnp.stack([child_tile[None]] * lax.axis_size(('row', 'col'...]
    all_gather x1 -> x0, waiting for transfers between devices: 102 us -> none  [body(): lax.all_gather(child_tile[None], ('row', 'col'), axis=0, tiled=True)]
    another operation x0 -> x2, local copies, waits for them, and re-layouts: none -> 29.5 us  [the longest x1 20.8 us: body(): incoming.reshape(piece_count, child_rows, BLK, child_cols, BLK)]
    reshape x1 -> x0, local copies, waits for them, and re-layouts: 20.8 us -> none  [body(): incoming.reshape(piece_count, child_rows, BLK, child_cols, BLK)]
  transfers between devices with their start and end apart: 14 -> 14, of which waited for: 14 -> 14; matrix products, arithmetic and copies ran while one was open for 1% -> 0% of each run, Pallas kernels for 0% -> 0%
where the time goes in v1:
time: 1870 us
  waiting for transfers between devices  1530 us (82%)
  other arithmetic  217 us (12%)
  local copies, waits for them, and re-layouts  64.4 us (3%)
  matrix products  23.1 us (1%)
    psum x12, waiting for transfers between devices, broadcast(): return lax.psum(kept, axis)  1110 us
    all_to_all x1, waiting for transfers between devices, body(): lax.all_to_all(jnp.stack([child_tile[None]] * lax.axis_size(('row', 'col'...  368 us
    another operation x18, other arithmetic, body(): pivot_factor = jnp.linalg.cholesky(share_diagonal)  74.3 us
    another operation x12, other arithmetic, body(): jax.scipy.linalg.solve_triangular(pivot_factor, share_col_panel.T, lower=...  62.8 us
    reduce_scatter x1, waiting for transfers between devices, body(): lax.psum_scatter(spread_sum, 'sub', scatter_dimension=1, tiled=True)  51.3 us
    scatter-add x1, other arithmetic, body(): zero_carry.at[row_target[:, :, None], :, col_target[:, None, :], :]  49.3 us
  transfers between devices with their start and end apart: 14, of which 14 were waited for; matrix products, arithmetic and copies ran while one was open for 0% of the time, Pallas kernels for 0%

profile of v1, /device:TPU:2, one launch (start us, length us, event | category | flops | bytes accessed | tf_op | source)
XLA Modules:
  0.0 1865.1 jit_solution(10285731017699056300)
XLA Ops:
  6.5 8.7 stack.3
  15.2 12.3 all-to-all-start
  28.6 367.7 %all-to-all-done = f32[64,1,256,256]{3,2,1,0:T(8,128)} async-done(((f32[64,1,256,256]{3,2,1,0:T(8,128)}), f32[64,1,256,256]{3,2,1,0:T(8,128)}, u32[]{:S(2)}, u32[]{:S(2)}) %all-to-all-start) | async-done | bytes 16777248 | tf_op jit(solution)/shard_map/all_to_all | solution.py:38
  396.4 20.8 %reshape_reshape.3 = f32[64,2,128,2,128]{4,3,2,1,0:T(2,128)} reshape(f32[64,1,256,256]{3,2,1,0:T(8,128)} %all-to-all-done) | data formatting | bytes 33554432 | tf_op jit(solution)/shard_map/reshape;reshape | solution.py:55
  417.2 12.6 copy.82
  432.2 49.3 %scatter_fusion = f32[8,128,8,128]{3,1,2,0:T(8,128)} fusion(f32[8,128,8,128]{3,1,2,0:T(8,128)} %broadcast_in_dim.231, s32[256]{0:T(256)S(1)} %reshape.467, f32[256,128,128]{2,1,0:T(8,128)} %bitcast.195), kind=kCustom, calls=%fused_computation | custom fusion | flops 4194304 | bytes 50333696 | tf_op jit(solution)/shard_map/scatter-add | solution.py:58
  481.5 5.5 copy.83
  493.5 51.3 %reduce-scatter.2.cloned.1.call-done = f32[1024,256]{0,1:T(8,128)} async-done(((f32[1024,1024]{0,1:T(8,128)}), f32[1024,256]{0,1:T(8,128)}) %reduce-scatter.2.cloned.1.call-update) | async-done | bytes 1048592 | tf_op jit(solution)/shard_map/reduce_scatter | solution.py:62
  548.4 113.1 %all-reduce.19.cloned.1.call-done = f32[1024,128]{0,1:T(8,128)} async-done(((f32[1024,128]{0,1:T(8,128)}), f32[1024,128]{0,1:T(8,128)}) %all-reduce.19.cloned.1.call-update) | async-done | bytes 524304 | tf_op jit(solution)/shard_map/psum | solution.py:13
  663.3 73.7 %all-reduce.41.cloned.1.call-done = (f32[128,256]{0,1:T(8,128)}, f32[128,128]{0,1:T(8,128)}) async-done(((f32[128,256]{0,1:T(8,128)}, f32[128,128]{0,1:T(8,128)}), (f32[128,256]{0,1:T(8,128)}, f32[128,128]{0,1:T(8,128)})) %all-reduce.41.cloned.1.call-update) | async-done | bytes 196624 | tf_op jit(solution)/shard_map/psum | solution.py:13
  738.9 11.7 cholesky.104
  751.9 9.8 custom-call.20
  768.0 111.7 %all-reduce.21.cloned.1.call-done = f32[1024,128]{0,1:T(8,128)} async-done(((f32[1024,128]{0,1:T(8,128)}), f32[1024,128]{0,1:T(8,128)}) %all-reduce.21.cloned.1.call-update) | async-done | bytes 524304 | tf_op jit(solution)/shard_map/psum | solution.py:13
  881.5 73.5 %all-reduce.39.cloned.1.call-done = (f32[128,256]{0,1:T(8,128)}, f32[128,128]{0,1:T(8,128)}) async-done(((f32[128,256]{0,1:T(8,128)}, f32[128,128]{0,1:T(8,128)}), (f32[128,256]{0,1:T(8,128)}, f32[128,128]{0,1:T(8,128)})) %all-reduce.39.cloned.1.call-update) | async-done | bytes 196624 | tf_op jit(solution)/shard_map/psum | solution.py:13
  956.8 11.7 cholesky.115
  969.9 9.8 custom-call.22
  985.9 111.7 %all-reduce.23.cloned.1.call-done = f32[1024,128]{0,1:T(8,128)} async-done(((f32[1024,128]{0,1:T(8,128)}), f32[1024,128]{0,1:T(8,128)}) %all-reduce.23.cloned.1.call-update) | async-done | bytes 524304 | tf_op jit(solution)/shard_map/psum | solution.py:13
  1099.5 73.6 %all-reduce.37.cloned.1.call-done = (f32[128,256]{0,1:T(8,128)}, f32[128,128]{0,1:T(8,128)}) async-done(((f32[128,256]{0,1:T(8,128)}, f32[128,128]{0,1:T(8,128)}), (f32[128,256]{0,1:T(8,128)}, f32[128,128]{0,1:T(8,128)})) %all-reduce.37.cloned.1.call-update) | async-done | bytes 196624 | tf_op jit(solution)/shard_map/psum | solution.py:13
  1174.9 11.7 cholesky.126
  1188.0 9.8 custom-call.24
  1204.1 111.7 %all-reduce.25.cloned.1.call-done = f32[1024,128]{0,1:T(8,128)} async-done(((f32[1024,128]{0,1:T(8,128)}), f32[1024,128]{0,1:T(8,128)}) %all-reduce.25.cloned.1.call-update) | async-done | bytes 524304 | tf_op jit(solution)/shard_map/psum | solution.py:13
  1317.9 73.4 %all-reduce.35.cloned.1.call-done = (f32[128,256]{0,1:T(8,128)}, f32[128,128]{0,1:T(8,128)}) async-done(((f32[128,256]{0,1:T(8,128)}, f32[128,128]{0,1:T(8,128)}), (f32[128,256]{0,1:T(8,128)}, f32[128,128]{0,1:T(8,128)})) %all-reduce.35.cloned.1.call-update) | async-done | bytes 196624 | tf_op jit(solution)/shard_map/psum | solution.py:13
  1393.1 11.7 cholesky.137
  1406.1 9.8 custom-call.26
  1422.2 111.6 %all-reduce.27.cloned.1.call-done = f32[1024,128]{0,1:T(8,128)} async-done(((f32[1024,128]{0,1:T(8,128)}), f32[1024,128]{0,1:T(8,128)}) %all-reduce.27.cloned.1.call-update) | async-done | bytes 524304 | tf_op jit(solution)/shard_map/psum | solution.py:13
  1535.7 73.7 %all-reduce.33.cloned.1.call-done = (f32[128,256]{0,1:T(8,128)}, f32[128,128]{0,1:T(8,128)}) async-done(((f32[128,256]{0,1:T(8,128)}, f32[128,128]{0,1:T(8,128)}), (f32[128,256]{0,1:T(8,128)}, f32[128,128]{0,1:T(8,128)})) %all-reduce.33.cloned.1.call-update) | async-done | bytes 196624 | tf_op jit(solution)/shard_map/psum | solution.py:13
  1611.2 11.7 cholesky.148
  1624.2 9.8 custom-call.28
  1640.5 111.5 %all-reduce.29.cloned.1.call-done = f32[1024,128]{0,1:T(8,128)} async-done(((f32[1024,128]{0,1:T(8,128)}), f32[1024,128]{0,1:T(8,128)}) %all-reduce.29.cloned.1.call-update) | async-done | bytes 524304 | tf_op jit(solution)/shard_map/psum | solution.py:13
  1753.6 73.9 %all-reduce.31.cloned.1.call-done = (f32[128,256]{0,1:T(8,128)}, f32[128,128]{0,1:T(8,128)}) async-done(((f32[128,256]{0,1:T(8,128)}, f32[128,128]{0,1:T(8,128)}), (f32[128,256]{0,1:T(8,128)}, f32[128,128]{0,1:T(8,128)})) %all-reduce.31.cloned.1.call-update) | async-done | bytes 196624 | tf_op jit(solution)/shard_map/psum | solution.py:13
  1829.3 11.7 cholesky.159
  1842.4 9.8 custom-call.30
  (151 shorter events, 80.4 us)
Async XLA Ops:
  15.2 12.5 copy-start.1
  15.2 381.1 %all-to-all-start = ((f32[64,1,256,256]{3,2,1,0:T(8,128)}), f32[64,1,256,256]{3,2,1,0:T(8,128)}, u32[]{:S(2)}, u32[]{:S(2)}) async-start(f32[64,1,256,256]{3,2,1,0:T(8,128)} %stack.3), calls=%async_computation | async-start | bytes 33554432 | tf_op jit(solution)/shard_map/all_to_all | solution.py:38
  27.6 517.2 %reduce-scatter.2.cloned.1.call-start = ((), (), s32[]{:S(2)}) async-start(), calls=%async_computation.2 | async-start | bytes 5242880 | tf_op jit(solution)/shard_map/reduce_scatter | solution.py:62
  481.5 10.7 copy-start
  492.2 169.4 %all-reduce.19.cloned.1.call-start = ((), (), s32[]{:S(2)}) async-start(), calls=%async_computation.3 | async-start | bytes 1048576 | tf_op jit(solution)/shard_map/psum | solution.py:13
  547.0 190.1 %all-reduce.41.cloned.1.call-start = ((), (), s32[]{:S(2)}) async-start(), calls=%async_computation.14 | async-start | bytes 393216 | tf_op jit(solution)/shard_map/psum | solution.py:13
  663.0 216.6 %all-reduce.21.cloned.1.call-start = ((), (), s32[]{:S(2)}) async-start(), calls=%async_computation.4 | async-start | bytes 1048576 | tf_op jit(solution)/shard_map/psum | solution.py:13
  767.2 187.8 %all-reduce.39.cloned.1.call-start = ((), (), s32[]{:S(2)}) async-start(), calls=%async_computation.13 | async-start | bytes 393216 | tf_op jit(solution)/shard_map/psum | solution.py:13
  881.2 216.5 %all-reduce.23.cloned.1.call-start = ((), (), s32[]{:S(2)}) async-start(), calls=%async_computation.5 | async-start | bytes 1048576 | tf_op jit(solution)/shard_map/psum | solution.py:13
  985.2 188.0 %all-reduce.37.cloned.1.call-start = ((), (), s32[]{:S(2)}) async-start(), calls=%async_computation.12 | async-start | bytes 393216 | tf_op jit(solution)/shard_map/psum | solution.py:13
  1099.1 216.6 %all-reduce.25.cloned.1.call-start = ((), (), s32[]{:S(2)}) async-start(), calls=%async_computation.6 | async-start | bytes 1048576 | tf_op jit(solution)/shard_map/psum | solution.py:13
  1203.3 188.0 %all-reduce.35.cloned.1.call-start = ((), (), s32[]{:S(2)}) async-start(), calls=%async_computation.11 | async-start | bytes 393216 | tf_op jit(solution)/shard_map/psum | solution.py:13
  1317.3 216.6 %all-reduce.27.cloned.1.call-start = ((), (), s32[]{:S(2)}) async-start(), calls=%async_computation.7 | async-start | bytes 1048576 | tf_op jit(solution)/shard_map/psum | solution.py:13
  1421.5 187.9 %all-reduce.33.cloned.1.call-start = ((), (), s32[]{:S(2)}) async-start(), calls=%async_computation.10 | async-start | bytes 393216 | tf_op jit(solution)/shard_map/psum | solution.py:13
  1535.4 216.6 %all-reduce.29.cloned.1.call-start = ((), (), s32[]{:S(2)}) async-start(), calls=%async_computation.8 | async-start | bytes 1048576 | tf_op jit(solution)/shard_map/psum | solution.py:13
  1639.5 188.0 %all-reduce.31.cloned.1.call-start = ((), (), s32[]{:S(2)}) async-start(), calls=%async_computation.9 | async-start | bytes 393216 | tf_op jit(solution)/shard_map/psum | solution.py:13
Sparse Core Ops, SparseCore 0:
  492.3 52.4 reduce-scatter.1
  548.0 113.5 all-reduce.18
  663.9 73.0 all-reduce.40
  767.4 112.2 all-reduce.20
  881.9 73.0 all-reduce.38
  985.3 112.2 all-reduce.22
  1100.0 73.0 all-reduce.36
  1203.4 112.2 all-reduce.24
  1318.2 73.0 all-reduce.34
  1421.6 112.2 all-reduce.26
  1536.2 73.0 all-reduce.32
  1639.7 112.2 all-reduce.28
  1754.4 73.0 all-reduce.30
